TPU v7x, 32 devices: a whole 2x2x4 slice. The times are simulated.
32 devices in a mesh: branch: 2 (over x), tok: 16 (over z, y, core).
Axes of the slice: x: 2, y: 2, z: 4, core: 2. Of those that a mesh axis runs over, the one named last changes fastest.
Arguments:
- teacher_hidden: bfloat16 [2, 256, 4096], P('branch', 'tok'), may hold values from -400 to 400
- teacher_gain: float32 [2, 4096], P('branch'), may hold values from 0.5 to 1.5
- teacher_head: bfloat16 [2, 4096, 20480], P('branch', None, 'tok'), may hold values from -30 to 30
- student_hidden: bfloat16 [256, 4096], P('branch'), may hold values from -400 to 400
- student_gain: float32 [4096], replicated, may hold values from 0.5 to 1.5
- student_head: bfloat16 [4096, 20480], P('branch', 'tok'), may hold values from -30 to 30
- cluster_weights: int32 [256, 2], P(None, 'branch'), may hold values from 0 to 64, as said below
- token_ids: int32 [256], P('branch'), may hold values from 0 to 20479
Outputs:
- grad_head: float32 [4096, 20480], P('branch', 'tok')
- grad_hidden: float32 [256, 4096], P('branch', 'tok')
- grad_gain: float32 [4096], P('tok')
Inputs may be any that keep to these rules, and one draw needn't show every extreme that they name: `cluster_weights`: each token's 2 weights sum to 64.
All inputs are finite; a program needn't handle non-finite values.
Results may differ from a plain program's by a relative error of at most 0.0063.
Values may be sent and summed in bfloat16 or wider, within the bound.
No kernel may reach another device: no remote copies, remote signals or barrier semaphores. Data moves between devices by JAX's collectives and lax.ppermute only.
A program may use at most 128 MiB of HBM per device.

v0:
```python
import jax
import jax.numpy as jnp
from jax import lax
from jax.sharding import PartitionSpec as P

DEN = 64
eps = 1e-05
mix_label = 0.25
loss_scale = 64.0


def merged(value, axis, combine):
    everything = jax.tree.map(lambda part: lax.all_gather(part, axis), value)
    leading = jax.tree.map(lambda part: part[0], everything)

    def step(k, so_far):
        return combine(so_far, jax.tree.map(lambda part: part[k], everything))

    return lax.fori_loop(1, lax.axis_size(axis), step, leading)


def normalize(hidden, gain):
    values = hidden.astype(jnp.float32)
    inv_scale = lax.rsqrt(jnp.mean(values * values, axis=-1, keepdims=True) + eps)
    return ((values * inv_scale * gain).astype(jnp.bfloat16), inv_scale)


def combine_stats(first, second):
    top = jnp.maximum(first[0], second[0])
    return (top, first[1] * jnp.exp(first[0] - top) + second[1] * jnp.exp(second[0] - top))


def probabilities(logits):
    local_max = jnp.max(logits, axis=1)
    local_scaled = jnp.exp(logits - local_max[:, None])
    row_max, row_total = merged((local_max, jnp.sum(local_scaled, axis=1)), "tok", combine_stats)
    scaled = local_scaled * jnp.exp(local_max - row_max)[:, None]
    return scaled / row_total[:, None]


def per_device(
    teacher_hidden,
    teacher_gain,
    teacher_head,
    student_hidden,
    student_gain,
    student_head,
    cluster_weights,
    token_ids,
):
    rows_here = student_hidden.shape[0]
    width = student_hidden.shape[1]
    head_cols = teacher_head.shape[2]
    branch_gain = teacher_gain[0]
    branch_head = teacher_head[0]
    normed, unused_scale = normalize(
        lax.all_gather(teacher_hidden[0], "tok", axis=0, tiled=True), branch_gain
    )
    teacher_logits = jnp.dot(normed, branch_head, preferred_element_type=jnp.float32)
    weight = cluster_weights[:, 0].astype(jnp.float32) / DEN
    terms = probabilities(teacher_logits) * weight[:, None]
    mixed_all = lax.psum(terms, "branch")
    mixed = lax.dynamic_slice_in_dim(mixed_all, lax.axis_index("branch") * rows_here, rows_here, 0)
    student_normed, inv_scale = normalize(student_hidden, student_gain)
    student_logits = jnp.dot(
        student_normed,
        lax.all_gather(student_head, "branch", axis=0, tiled=True),
        preferred_element_type=jnp.float32,
    )
    student_probs = probabilities(student_logits)
    offset = lax.axis_index("tok") * head_cols
    onehot = (
        token_ids[:, None] == offset + jnp.arange(head_cols, dtype=jnp.int32)[None, :]
    ).astype(jnp.float32)
    targets = (1.0 - mix_label) * mixed + mix_label * onehot
    logit_grads = (loss_scale * (student_probs - targets)).astype(jnp.bfloat16)
    contract = (((1,), (1,)), ((), ()))
    partial_grads = lax.dot_general(
        logit_grads,
        lax.all_gather(student_head, "branch", axis=0, tiled=True),
        contract,
        preferred_element_type=jnp.float32,
    )
    normed_grads = lax.psum_scatter(partial_grads, "tok", scatter_dimension=1, tiled=True)
    slice_width = normed_grads.shape[1]
    col_start = lax.axis_index("tok") * slice_width
    hidden_cols = lax.dynamic_slice_in_dim(student_hidden, col_start, slice_width, 1).astype(
        jnp.float32
    )
    gain_cols = lax.dynamic_slice_in_dim(student_gain, col_start, slice_width, 0)
    grad_gain = lax.psum(jnp.sum(normed_grads * hidden_cols * inv_scale, axis=0), "branch")
    row_dots = lax.psum(jnp.sum(gain_cols[None, :] * normed_grads * hidden_cols, axis=1), "tok")
    grad_hidden = (
        inv_scale * gain_cols[None, :] * normed_grads
        - hidden_cols * inv_scale**3 * row_dots[:, None] / width
    )
    exchanged = lax.all_to_all(student_normed, "branch", split_axis=1, concat_axis=0, tiled=True)
    all_grads = lax.all_gather(logit_grads, "branch", axis=0, tiled=True)
    grad_head = lax.dot_general(
        exchanged, all_grads, (((0,), (0,)), ((), ())), preferred_element_type=jnp.float32
    )
    return (grad_head, grad_hidden, grad_gain)


def solution(mesh):
    in_specs = (
        P("branch", "tok", None),
        P("branch", None),
        P("branch", None, "tok"),
        P("branch", None),
        P(),
        P("branch", "tok"),
        P(None, "branch"),
        P("branch"),
    )
    out_specs = (P("branch", "tok"), P("branch", "tok"), P("tok"))
    return jax.shard_map(
        per_device, mesh=mesh, in_specs=in_specs, out_specs=out_specs, check_vma=False
    )
```

profile of v0, /device:TPU:0, one launch (start us, length us, event | category | flops | bytes accessed | tf_op | source)
XLA Modules:
  0.0 349.2 jit_solution(5427056235205396135)
XLA Ops:
  10.4 1.6 fusion.9
  12.0 42.4 %all-gather.14.cloned.1.call-done = bf16[1,256,4096]{2,1,0:T(8,128)(2,1)} async-done(((bf16[1,16,4096]{2,1,0:T(8,128)(2,1)}), bf16[1,256,4096]{2,1,0:T(8,128)(2,1)}) %all-gather.14.cloned.1.call-update) | async-done | bytes 2097168 | tf_op jit(solution)/shard_map/all_gather | solution.py:57
  54.4 2.2 fusion.4
  56.6 7.1 %fusion.22 = (f32[256]{0:T(256)S(1)}, f32[256,1280]{1,0:T(8,128)S(1)}) fusion(bf16[1,4096,1280]{2,1,0:T(8,128)(2,1)} %param.14, bf16[1,256,4096]{2,1,0:T(8,128)(2,1)S(1)} %copy-done, f32[4096]{0:T(1024)S(1)} %bitcast.78, f32[256]{0:T(256)S(1)} %add_rsqrt_fusion), kind=kOutput, calls=%fused_computation.50 | convolution fusion | flops 2688876288 | bytes 13912064 | tf_op jit(solution)/shard_map/dot_general | solution.py:59
  64.0 19.1 %all-gather.8 = f32[16,1,256]{2,1,0:T(1,128)S(1)} all-gather(f32[1,1,256]{2,1,0:T(1,128)S(1)} %bitcast.76), channel_id=6, replica_groups=mesh['branch'=2,'tok'=16] {'tok'}, dimensions={0}, use_global_device_ids=true | all-gather | bytes 17408 | tf_op jit(solution)/shard_map/all_gather | solution.py:13
  83.1 17.4 %all-gather.7 = f32[16,1,256]{2,1,0:T(1,128)S(1)} all-gather(f32[1,1,256]{2,1,0:T(1,128)S(1)} %bitcast.71), channel_id=5, replica_groups=mesh['branch'=2,'tok'=16] {'tok'}, dimensions={0}, use_global_device_ids=true | all-gather | bytes 17408 | tf_op jit(solution)/shard_map/all_gather | solution.py:13
  100.6 0.8 while.35
  101.4 1.4 divide_multiply_fusion
  102.9 81.2 %all-gather.12.cloned.1.call-done = bf16[4096,1280]{1,0:T(8,128)(2,1)} async-done(((bf16[2048,1280]{1,0:T(8,128)(2,1)}), bf16[4096,1280]{1,0:T(8,128)(2,1)}) %all-gather.12.cloned.1.call-update) | async-done | bytes 10485776 | tf_op jit(solution)/shard_map/all_gather | solution.py:67
  184.1 6.0 %fusion.23 = (f32[128]{0:T(128)S(1)}, f32[128,1280]{1,0:T(8,128)S(1)}) fusion(bf16[128,4096]{0,1:T(8,128)(2,1)} %fusion.9, bf16[4096,1280]{1,0:T(8,128)(2,1)} %all-gather.12.cloned.1.call-done), kind=kOutput, calls=%fused_computation.51 | convolution fusion | flops 1342340992 | bytes 12190208 | tf_op jit(solution)/shard_map/dot_general | solution.py:65
  190.4 21.3 %all-gather.6 = f32[16,1,128]{2,1,0:T(1,128)S(1)} all-gather(f32[1,1,128]{2,1,0:T(1,128)S(1)} %bitcast.77), channel_id=3, replica_groups=mesh['branch'=2,'tok'=16] {'tok'}, dimensions={0}, use_global_device_ids=true | all-gather | bytes 8704 | tf_op jit(solution)/shard_map/all_gather | solution.py:13
  211.7 17.4 %all-gather.5 = f32[16,1,128]{2,1,0:T(1,128)S(1)} all-gather(f32[1,1,128]{2,1,0:T(1,128)S(1)} %bitcast.74), channel_id=2, replica_groups=mesh['branch'=2,'tok'=16] {'tok'}, dimensions={0}, use_global_device_ids=true | all-gather | bytes 8704 | tf_op jit(solution)/shard_map/all_gather | solution.py:13
  229.8 3.1 all-reduce.2.cloned.1.call-done
  232.9 1.4 multiply_convert_fusion
  234.3 8.7 %fusion.25 = f32[128,4096]{1,0:T(8,128)} fusion(bf16[128,1280]{1,0:T(8,128)(2,1)S(1)} %multiply_convert_fusion, bf16[4096,1280]{1,0:T(8,128)(2,1)} %all-gather.12.cloned.1.call-done), kind=kOutput, calls=%fused_computation.53 | convolution fusion | flops 1342177280 | bytes 12910592 | tf_op jit(solution)/shard_map/dot_general | solution.py:78
  243.0 3.6 %all-to-all-start = ((bf16[128,2,2048]{0,2,1:T(8,128)(2,1)}), bf16[128,2,2048]{0,2,1:T(8,128)(2,1)S(1)}, u32[]{:S(2)}, u32[]{:S(2)}) async-start(bf16[128,2,2048]{0,2,1:T(8,128)(2,1)} %bitcast.4), calls=%async_computation | async-start | bytes 2097152 | tf_op jit(solution)/shard_map/all_to_all | solution.py:97
  246.7 13.6 %all-to-all-done = bf16[128,2,2048]{0,2,1:T(8,128)(2,1)S(1)} async-done(((bf16[128,2,2048]{0,2,1:T(8,128)(2,1)}), bf16[128,2,2048]{0,2,1:T(8,128)(2,1)S(1)}, u32[]{:S(2)}, u32[]{:S(2)}) %all-to-all-start) | async-done | bytes 1048608 | tf_op jit(solution)/shard_map/all_to_all | solution.py:97
  260.9 9.1 %all_gather.44 = bf16[256,1280]{1,0:T(8,128)(2,1)S(1)} all-gather(bf16[128,1280]{1,0:T(8,128)(2,1)S(1)} %multiply_convert_fusion), channel_id=1, replica_groups=mesh['branch'=2,'tok'=16] {'branch'}, dimensions={0}, use_global_device_ids=true | all-gather | bytes 983040 | tf_op jit(solution)/shard_map/all_gather | solution.py:98
  269.9 5.7 %fusion.24 = f32[2048,1280]{1,0:T(8,128)} fusion(bf16[256,2048]{1,0:T(8,128)(2,1)S(1)} %bitcast.63, bf16[256,1280]{1,0:T(8,128)(2,1)S(1)} %all_gather.44), kind=kOutput, calls=%fused_computation.52 | convolution fusion | flops 1342177280 | bytes 12189696 | tf_op jit(solution)/shard_map/dot_general | solution.py:99
  275.6 29.3 %reduce-scatter.2.cloned.1.call-done = f32[128,256]{1,0:T(8,128)} async-done(((f32[128,4096]{1,0:T(8,128)}), f32[128,256]{1,0:T(8,128)}) %reduce-scatter.2.cloned.1.call-update) | async-done | bytes 131088 | tf_op jit(solution)/shard_map/reduce_scatter | solution.py:84
  305.0 1.0 fusion.21
  306.0 29.5 %psum.22 = f32[128]{0:T(128)S(1)} all-reduce(f32[128]{0:T(128)S(1)} %get-tuple-element.274), channel_id=1, replica_groups=mesh['branch'=2,'tok'=16] {'tok'}, use_global_device_ids=true, to_apply=%region_13.0 | all-reduce | flops 128 | bytes 1024 | tf_op jit(solution)/shard_map/psum | solution.py:92
  335.5 5.5 %psum.23 = f32[256]{0:T(256)} all-reduce(f32[256]{0:T(256)S(1)} %get-tuple-element.273), channel_id=1, replica_groups=mesh['branch'=2,'tok'=16] {'branch'}, use_global_device_ids=true, to_apply=%region_15.0 | all-reduce | flops 256 | bytes 2048 | tf_op jit(solution)/shard_map/psum | solution.py:91
  341.0 1.7 fusion.18
  (84 shorter events, 6.0 us)
Async XLA Ops:
  7.2 47.2 %all-gather.14.cloned.1.call-start = ((), (), s32[]{:S(2)}) async-start(), calls=%async_computation.5 | async-start | bytes 2228224 | tf_op jit(solution)/shard_map/all_gather | solution.py:57
  7.9 1.2 copy-start.1
  7.9 176.2 %all-gather.12.cloned.1.call-start = ((), (), s32[]{:S(2)}) async-start(), calls=%async_computation.2 | async-start | bytes 15728640 | tf_op jit(solution)/shard_map/all_gather | solution.py:67
  8.7 1.7 copy-start.3
  8.7 1.7 copy-start.2
  8.7 224.2 %all-reduce.2.cloned.1.call-start = ((), (), s32[]{:S(2)}) async-start(), calls=%async_computation.3 | async-start | bytes 2621440 | tf_op jit(solution)/shard_map/psum | solution.py:62
  10.4 46.2 %copy-start.5 = (f32[1,4096]{1,0:T(1,128)S(1)}, f32[1,4096]{1,0:T(1,128)}, u32[]{:S(2)}) copy-start(f32[1,4096]{1,0:T(1,128)} %param.13) | copy-start | bytes 49156
  54.3 2.3 copy-start
  102.9 130.0 %copy-start.4 = (s32[128]{0:T(128)S(1)}, s32[128]{0:T(128)}, u32[]{:S(2)}) copy-start(s32[128]{0:T(128)} %param.19) | copy-start | bytes 1540
  102.9 202.1 %reduce-scatter.2.cloned.1.call-start = ((), (), s32[]{:S(2)}) async-start(), calls=%async_computation.4 | async-start | bytes 2228224 | tf_op jit(solution)/shard_map/reduce_scatter | solution.py:84
  243.0 17.3 %all-to-all-start = ((bf16[128,2,2048]{0,2,1:T(8,128)(2,1)}), bf16[128,2,2048]{0,2,1:T(8,128)(2,1)S(1)}, u32[]{:S(2)}, u32[]{:S(2)}) async-start(bf16[128,2,2048]{0,2,1:T(8,128)(2,1)} %bitcast.4), calls=%async_computation | async-start | bytes 2097152 | tf_op jit(solution)/shard_map/all_to_all | solution.py:97
Sparse Core Ops, SparseCore 0:
  10.1 44.1 all-gather.13
  55.9 128.1 all-gather.11
  187.0 45.8 all-reduce.1
  243.2 61.7 reduce-scatter.1
where the time goes:
time: 350 us; the launch traced here: 349 us
  waiting for transfers between devices  171 us (49%)
  blocking collectives  119 us (34%)
  matrix products  27.5 us (8%)
  between operations  13.9 us (4%)
  other arithmetic  11.2 us (3%)
  starting transfers between devices  3.75 us (1%)
    all_gather x1, waiting for transfers between devices, per_device(): lax.all_gather(student_head, 'branch', axis=0, tiled=True)  81.2 us
    all_gather x4, blocking collectives, merged(): everything = jax.tree.map(lambda part: lax.all_gather(part, axis), value)  75.3 us
    all_gather x1, waiting for transfers between devices, per_device(): lax.all_gather(teacher_hidden[0], 'tok', axis=0, tiled=True)  42.4 us
    psum x1, blocking collectives, per_device(): lax.psum(jnp.sum(gain_cols[None, :] * normed_grads * hidden_cols, axis=1)...  29.5 us
    reduce_scatter x1, waiting for transfers between devices, per_device(): lax.psum_scatter(partial_grads, 'tok', scatter_dimension=1, tiled=True)  29.3 us
    all_to_all x1, waiting for transfers between devices, per_device(): lax.all_to_all(student_normed, 'branch', split_axis=1, concat_axis=0, til...  13.6 us
    all_gather x1, blocking collectives, per_device(): all_grads = lax.all_gather(logit_grads, 'branch', axis=0, tiled=True)  9.09 us
    dot_general x1, matrix products, per_device(): lax.dot_general(logit_grads, lax.all_gather(student_head, 'branch', axis=...  8.73 us
  transfers between devices with their start and end apart: 5, of which 5 were waited for; matrix products, arithmetic and copies ran while one was open for 8% of the time, Pallas kernels for 0%

commit v1 on v0

--- a/solution.py
+++ b/solution.py
@@ -7,6 +7,22 @@
 eps = 1e-05
 mix_label = 0.25
 loss_scale = 64.0
+
+
+def measure_the_threads(vals):
+    z1 = lax.axis_size("tok")
+    new, earlier, response = (z1, lax.axis_index("tok"), vals.shape[0])
+    buffers = [p * new if pp == 0 else p for pp, p in enumerate(vals.shape)]
+    found_now = jnp.zeros(buffers, vals.dtype)
+    near = lax.dynamic_update_slice_in_dim(found_now, vals, earlier * response, axis=0)
+    for dev_i in range(1, new):
+        x_next = range(new)
+        all_values = map(lambda pp: (pp, (pp + 1) % new), x_next)
+        vals = lax.ppermute(vals, "tok", list(all_values))
+        near = lax.dynamic_update_slice_in_dim(
+            near, vals, (earlier - dev_i) % new * response, axis=0
+        )
+    return near
 
 
 def merged(value, axis, combine):
@@ -53,9 +69,7 @@
     head_cols = teacher_head.shape[2]
     branch_gain = teacher_gain[0]
     branch_head = teacher_head[0]
-    normed, unused_scale = normalize(
-        lax.all_gather(teacher_hidden[0], "tok", axis=0, tiled=True), branch_gain
-    )
+    normed, unused_scale = normalize(measure_the_threads(teacher_hidden[0]), branch_gain)
     teacher_logits = jnp.dot(normed, branch_head, preferred_element_type=jnp.float32)
     weight = cluster_weights[:, 0].astype(jnp.float32) / DEN
     terms = probabilities(teacher_logits) * weight[:, None]

time: 350 us -> 322 us (0.920)
  waiting for transfers between devices: 171 us -> 145 us
    ppermute x0 -> x15, waiting for transfers between devices: none -> 103 us  [measure_the_threads(): vals = lax.ppermute(vals, 'tok', list(all_values))]
    all_gather x1, waiting for transfers between devices: 81.2 us -> 0.02 us  [per_device(): lax.all_gather(student_head, 'branch', axis=0, tiled=True)]
    all_gather x1 -> x0, waiting for transfers between devices: 42.4 us -> none  [per_device(): lax.all_gather(teacher_hidden[0], 'tok', axis=0, tiled=True)]
  transfers between devices with their start and end apart: 5 -> 19, of which waited for: 5 -> 17; matrix products, arithmetic and copies ran while one was open for 8% -> 8% of each run, Pallas kernels for 0% -> 0%
where the time goes in v1:
time: 322 us; the launch traced here: 321 us
  waiting for transfers between devices  145 us (45%)
  blocking collectives  117 us (36%)
  matrix products  27.8 us (9%)
  between operations  14 us (4%)
  other arithmetic  9.47 us (3%)
  starting transfers between devices  4.29 us (1%)
    ppermute x15, waiting for transfers between devices, measure_the_threads(): vals = lax.ppermute(vals, 'tok', list(all_values))  103 us
    all_gather x4, blocking collectives, merged(): everything = jax.tree.map(lambda part: lax.all_gather(part, axis), value)  72.5 us
    psum x1, blocking collectives, per_device(): lax.psum(jnp.sum(gain_cols[None, :] * normed_grads * hidden_cols, axis=1)...  29.5 us
    reduce_scatter x1, waiting for transfers between devices, per_device(): lax.psum_scatter(partial_grads, 'tok', scatter_dimension=1, tiled=True)  27.6 us
    all_to_all x1, waiting for transfers between devices, per_device(): lax.all_to_all(student_normed, 'branch', split_axis=1, concat_axis=0, til...  14.5 us
    all_gather x1, blocking collectives, per_device(): all_grads = lax.all_gather(logit_grads, 'branch', axis=0, tiled=True)  9.95 us
    dot_general x1, matrix products, per_device(): lax.dot_general(logit_grads, lax.all_gather(student_head, 'branch', axis=...  8.75 us
    dot_general x1, matrix products, per_device(): jnp.dot(normed, branch_head, preferred_element_type=jnp.float32)  6.99 us
  transfers between devices with their start and end apart: 19, of which 17 were waited for; matrix products, arithmetic and copies ran while one was open for 8% of the time, Pallas kernels for 0%

profile of v1, /device:TPU:0, one launch (start us, length us, event | category | flops | bytes accessed | tf_op | source)
XLA Modules:
  0.0 321.3 jit_solution(14869688313189223548)
XLA Ops:
  15.6 7.1 %collective-permute-done.1 = bf16[16,4096]{1,0:T(8,128)(2,1)S(1)} collective-permute-done((bf16[16,4096]{1,0:T(8,128)(2,1)S(1)}, bf16[16,4096]{1,0:T(8,128)(2,1)S(1)}, u32[]{:S(2)}, u32[]{:S(2)}) %collective-permute-start.1) | collective-permute-done | bytes 131104 | tf_op jit(solution)/shard_map/ppermute | solution.py:21
  22.7 7.1 %collective-permute-done.2 = bf16[16,4096]{1,0:T(8,128)(2,1)S(1)} collective-permute-done((bf16[16,4096]{1,0:T(8,128)(2,1)S(1)}, bf16[16,4096]{1,0:T(8,128)(2,1)S(1)}, u32[]{:S(2)}, u32[]{:S(2)}) %collective-permute-start.2) | collective-permute-done | bytes 131104 | tf_op jit(solution)/shard_map/ppermute | solution.py:21
  29.8 7.1 %collective-permute-done.3 = bf16[16,4096]{1,0:T(8,128)(2,1)S(1)} collective-permute-done((bf16[16,4096]{1,0:T(8,128)(2,1)S(1)}, bf16[16,4096]{1,0:T(8,128)(2,1)S(1)}, u32[]{:S(2)}, u32[]{:S(2)}) %collective-permute-start.3) | collective-permute-done | bytes 131104 | tf_op jit(solution)/shard_map/ppermute | solution.py:21
  36.9 7.1 %collective-permute-done.4 = bf16[16,4096]{1,0:T(8,128)(2,1)S(1)} collective-permute-done((bf16[16,4096]{1,0:T(8,128)(2,1)S(1)}, bf16[16,4096]{1,0:T(8,128)(2,1)S(1)}, u32[]{:S(2)}, u32[]{:S(2)}) %collective-permute-start.4) | collective-permute-done | bytes 131104 | tf_op jit(solution)/shard_map/ppermute | solution.py:21
  44.0 7.1 %collective-permute-done.5 = bf16[16,4096]{1,0:T(8,128)(2,1)S(1)} collective-permute-done((bf16[16,4096]{1,0:T(8,128)(2,1)S(1)}, bf16[16,4096]{1,0:T(8,128)(2,1)S(1)}, u32[]{:S(2)}, u32[]{:S(2)}) %collective-permute-start.5) | collective-permute-done | bytes 131104 | tf_op jit(solution)/shard_map/ppermute | solution.py:21
  51.1 7.1 %collective-permute-done.6 = bf16[16,4096]{1,0:T(8,128)(2,1)S(1)} collective-permute-done((bf16[16,4096]{1,0:T(8,128)(2,1)S(1)}, bf16[16,4096]{1,0:T(8,128)(2,1)S(1)}, u32[]{:S(2)}, u32[]{:S(2)}) %collective-permute-start.6) | collective-permute-done | bytes 131104 | tf_op jit(solution)/shard_map/ppermute | solution.py:21
  58.2 7.1 %collective-permute-done.7 = bf16[16,4096]{1,0:T(8,128)(2,1)S(1)} collective-permute-done((bf16[16,4096]{1,0:T(8,128)(2,1)S(1)}, bf16[16,4096]{1,0:T(8,128)(2,1)S(1)}, u32[]{:S(2)}, u32[]{:S(2)}) %collective-permute-start.7) | collective-permute-done | bytes 131104 | tf_op jit(solution)/shard_map/ppermute | solution.py:21
  65.3 7.1 %collective-permute-done.8 = bf16[16,4096]{1,0:T(8,128)(2,1)S(1)} collective-permute-done((bf16[16,4096]{1,0:T(8,128)(2,1)S(1)}, bf16[16,4096]{1,0:T(8,128)(2,1)S(1)}, u32[]{:S(2)}, u32[]{:S(2)}) %collective-permute-start.8) | collective-permute-done | bytes 131104 | tf_op jit(solution)/shard_map/ppermute | solution.py:21
  72.4 7.1 %collective-permute-done.9 = bf16[16,4096]{1,0:T(8,128)(2,1)S(1)} collective-permute-done((bf16[16,4096]{1,0:T(8,128)(2,1)S(1)}, bf16[16,4096]{1,0:T(8,128)(2,1)S(1)}, u32[]{:S(2)}, u32[]{:S(2)}) %collective-permute-start.9) | collective-permute-done | bytes 131104 | tf_op jit(solution)/shard_map/ppermute | solution.py:21
  79.4 7.1 %collective-permute-done.10 = bf16[16,4096]{1,0:T(8,128)(2,1)S(1)} collective-permute-done((bf16[16,4096]{1,0:T(8,128)(2,1)S(1)}, bf16[16,4096]{1,0:T(8,128)(2,1)S(1)}, u32[]{:S(2)}, u32[]{:S(2)}) %collective-permute-start.10) | collective-permute-done | bytes 131104 | tf_op jit(solution)/shard_map/ppermute | solution.py:21
  86.5 7.1 %collective-permute-done.11 = bf16[16,4096]{1,0:T(8,128)(2,1)S(1)} collective-permute-done((bf16[16,4096]{1,0:T(8,128)(2,1)S(1)}, bf16[16,4096]{1,0:T(8,128)(2,1)S(1)}, u32[]{:S(2)}, u32[]{:S(2)}) %collective-permute-start.11) | collective-permute-done | bytes 131104 | tf_op jit(solution)/shard_map/ppermute | solution.py:21
  93.6 7.1 %collective-permute-done.12 = bf16[16,4096]{1,0:T(8,128)(2,1)S(1)} collective-permute-done((bf16[16,4096]{1,0:T(8,128)(2,1)S(1)}, bf16[16,4096]{1,0:T(8,128)(2,1)S(1)}, u32[]{:S(2)}, u32[]{:S(2)}) %collective-permute-start.12) | collective-permute-done | bytes 131104 | tf_op jit(solution)/shard_map/ppermute | solution.py:21
  100.7 7.1 %collective-permute-done.13 = bf16[16,4096]{1,0:T(8,128)(2,1)S(1)} collective-permute-done((bf16[16,4096]{1,0:T(8,128)(2,1)S(1)}, bf16[16,4096]{1,0:T(8,128)(2,1)S(1)}, u32[]{:S(2)}, u32[]{:S(2)}) %collective-permute-start.13) | collective-permute-done | bytes 131104 | tf_op jit(solution)/shard_map/ppermute | solution.py:21
  107.8 7.1 %collective-permute-done.14 = bf16[16,4096]{1,0:T(8,128)(2,1)S(1)} collective-permute-done((bf16[16,4096]{1,0:T(8,128)(2,1)S(1)}, bf16[16,4096]{1,0:T(8,128)(2,1)S(1)}, u32[]{:S(2)}, u32[]{:S(2)}) %collective-permute-start.14) | collective-permute-done | bytes 131104 | tf_op jit(solution)/shard_map/ppermute | solution.py:21
  115.4 7.0 %fusion.21 = (f32[256]{0:T(256)S(1)}, f32[256,1280]{1,0:T(8,128)S(1)}) fusion(bf16[1,4096,1280]{2,1,0:T(8,128)(2,1)} %param.14, bf16[256,4096]{1,0:T(8,128)(2,1)S(1)} %constant_dynamic-update-slice_fusion, f32[4096]{0:T(1024)S(1)} %bitcast.72, f32[256]{0:T(256)S(1)} %add_rsqrt_fusion), kind=kOutput, calls=%fused_computation.65 | convolution fusion | flops 2688876288 | bytes 13912064 | tf_op jit(solution)/shard_map/dot_general | solution.py:73
  122.7 17.2 %all-gather.7 = f32[16,1,256]{2,1,0:T(1,128)S(1)} all-gather(f32[1,1,256]{2,1,0:T(1,128)S(1)} %bitcast.70), channel_id=5, replica_groups=mesh['branch'=2,'tok'=16] {'tok'}, dimensions={0}, use_global_device_ids=true | all-gather | bytes 17408 | tf_op jit(solution)/shard_map/all_gather | solution.py:29
  139.9 19.1 %all-gather.6 = f32[16,1,256]{2,1,0:T(1,128)S(1)} all-gather(f32[1,1,256]{2,1,0:T(1,128)S(1)} %bitcast.65), channel_id=4, replica_groups=mesh['branch'=2,'tok'=16] {'tok'}, dimensions={0}, use_global_device_ids=true | all-gather | bytes 17408 | tf_op jit(solution)/shard_map/all_gather | solution.py:29
  168.1 17.4 %all-gather.5 = f32[16,1,128]{2,1,0:T(1,128)S(1)} all-gather(f32[1,1,128]{2,1,0:T(1,128)S(1)} %bitcast.71), channel_id=3, replica_groups=mesh['branch'=2,'tok'=16] {'tok'}, dimensions={0}, use_global_device_ids=true | all-gather | bytes 8704 | tf_op jit(solution)/shard_map/all_gather | solution.py:29
  185.5 18.8 %all-gather.4 = f32[16,1,128]{2,1,0:T(1,128)S(1)} all-gather(f32[1,1,128]{2,1,0:T(1,128)S(1)} %bitcast.68), channel_id=2, replica_groups=mesh['branch'=2,'tok'=16] {'tok'}, dimensions={0}, use_global_device_ids=true | all-gather | bytes 8704 | tf_op jit(solution)/shard_map/all_gather | solution.py:29
  206.4 8.8 %fusion.24 = f32[128,4096]{1,0:T(8,128)} fusion(bf16[128,1280]{1,0:T(8,128)(2,1)S(1)} %multiply_convert_fusion, bf16[4096,1280]{1,0:T(8,128)(2,1)} %all-gather.10.cloned.1.call-done), kind=kOutput, calls=%fused_computation.68 | convolution fusion | flops 1342177280 | bytes 12910592 | tf_op jit(solution)/shard_map/dot_general | solution.py:92
  218.9 14.5 %all-to-all-done = bf16[128,2,2048]{0,2,1:T(8,128)(2,1)S(1)} async-done(((bf16[128,2,2048]{0,2,1:T(8,128)(2,1)}), bf16[128,2,2048]{0,2,1:T(8,128)(2,1)S(1)}, u32[]{:S(2)}, u32[]{:S(2)}) %all-to-all-start) | async-done | bytes 1048608 | tf_op jit(solution)/shard_map/all_to_all | solution.py:111
  233.9 9.9 %all_gather.40 = bf16[256,1280]{1,0:T(8,128)(2,1)S(1)} all-gather(bf16[128,1280]{1,0:T(8,128)(2,1)S(1)} %multiply_convert_fusion), channel_id=1, replica_groups=mesh['branch'=2,'tok'=16] {'branch'}, dimensions={0}, use_global_device_ids=true | all-gather | bytes 983040 | tf_op jit(solution)/shard_map/all_gather | solution.py:112
  249.5 27.6 %reduce-scatter.2.cloned.1.call-done = f32[128,256]{1,0:T(8,128)} async-done(((f32[128,4096]{1,0:T(8,128)}), f32[128,256]{1,0:T(8,128)}) %reduce-scatter.2.cloned.1.call-update) | async-done | bytes 131088 | tf_op jit(solution)/shard_map/reduce_scatter | solution.py:98
  278.2 29.5 %psum.22 = f32[128]{0:T(128)S(1)} all-reduce(f32[128]{0:T(128)S(1)} %get-tuple-element.274), channel_id=1, replica_groups=mesh['branch'=2,'tok'=16] {'tok'}, use_global_device_ids=true, to_apply=%region_13.14 | all-reduce | flops 128 | bytes 1024 | tf_op jit(solution)/shard_map/psum | solution.py:106
  (128 shorter events, 39.5 us)
Async XLA Ops:
  7.2 154.2 %all-gather.10.cloned.1.call-start = ((), (), s32[]{:S(2)}) async-start(), calls=%async_computation.2 | async-start | bytes 15728640 | tf_op jit(solution)/shard_map/all_gather | solution.py:81
  7.2 1.2 copy-start
  7.2 8.4 %collective-permute-start = (bf16[16,4096]{1,0:T(8,128)(2,1)}, bf16[16,4096]{1,0:T(8,128)(2,1)S(1)}, u32[]{:S(2)}, u32[]{:S(2)}) collective-permute-start(bf16[16,4096]{1,0:T(8,128)(2,1)} %bitcast.58), channel_id=1, source_target_pairs={{0,1},{1,2},{2,3},{3,4},{4,5},{5,6},{6,7},{7,8},{8,9},{9,10},{10,1... | collective-permute-start | bytes 393224 | tf_op jit(solution)/shard_map/ppermute | solution.py:21
  7.9 197.1 %all-reduce.2.cloned.1.call-start = ((), (), s32[]{:S(2)}) async-start(), calls=%async_computation.3 | async-start | bytes 2621440 | tf_op jit(solution)/shard_map/psum | solution.py:76
  9.1 0.9 copy-start.2
  9.7 1.9 copy-start.3
  15.6 7.1 %collective-permute-start.1 = (bf16[16,4096]{1,0:T(8,128)(2,1)S(1)}, bf16[16,4096]{1,0:T(8,128)(2,1)S(1)}, u32[]{:S(2)}, u32[]{:S(2)}) collective-permute-start(bf16[16,4096]{1,0:T(8,128)(2,1)S(1)} %collective-permute-done), channel_id=1, source_target_pairs={{0,1},{1,2},{2,3},{3,4},{4,5},{5,6},{6,7},{7,8},{8,9},{9,10},{10,1... | collective-permute-start | bytes 393224 | tf_op jit(solution)/shard_map/ppermute | solution.py:21
  22.7 7.1 %collective-permute-start.2 = (bf16[16,4096]{1,0:T(8,128)(2,1)S(1)}, bf16[16,4096]{1,0:T(8,128)(2,1)S(1)}, u32[]{:S(2)}, u32[]{:S(2)}) collective-permute-start(bf16[16,4096]{1,0:T(8,128)(2,1)S(1)} %collective-permute-done.1), channel_id=1, source_target_pairs={{0,1},{1,2},{2,3},{3,4},{4,5},{5,6},{6,7},{7,8},{8,9},{9,10},{10,1... | collective-permute-start | bytes 393224 | tf_op jit(solution)/shard_map/ppermute | solution.py:21
  29.8 7.1 %collective-permute-start.3 = (bf16[16,4096]{1,0:T(8,128)(2,1)S(1)}, bf16[16,4096]{1,0:T(8,128)(2,1)S(1)}, u32[]{:S(2)}, u32[]{:S(2)}) collective-permute-start(bf16[16,4096]{1,0:T(8,128)(2,1)S(1)} %collective-permute-done.2), channel_id=1, source_target_pairs={{0,1},{1,2},{2,3},{3,4},{4,5},{5,6},{6,7},{7,8},{8,9},{9,10},{10,1... | collective-permute-start | bytes 393224 | tf_op jit(solution)/shard_map/ppermute | solution.py:21
  36.9 7.1 %collective-permute-start.4 = (bf16[16,4096]{1,0:T(8,128)(2,1)S(1)}, bf16[16,4096]{1,0:T(8,128)(2,1)S(1)}, u32[]{:S(2)}, u32[]{:S(2)}) collective-permute-start(bf16[16,4096]{1,0:T(8,128)(2,1)S(1)} %collective-permute-done.3), channel_id=1, source_target_pairs={{0,1},{1,2},{2,3},{3,4},{4,5},{5,6},{6,7},{7,8},{8,9},{9,10},{10,1... | collective-permute-start | bytes 393224 | tf_op jit(solution)/shard_map/ppermute | solution.py:21
  44.0 7.1 %collective-permute-start.5 = (bf16[16,4096]{1,0:T(8,128)(2,1)S(1)}, bf16[16,4096]{1,0:T(8,128)(2,1)S(1)}, u32[]{:S(2)}, u32[]{:S(2)}) collective-permute-start(bf16[16,4096]{1,0:T(8,128)(2,1)S(1)} %collective-permute-done.4), channel_id=1, source_target_pairs={{0,1},{1,2},{2,3},{3,4},{4,5},{5,6},{6,7},{7,8},{8,9},{9,10},{10,1... | collective-permute-start | bytes 393224 | tf_op jit(solution)/shard_map/ppermute | solution.py:21
  51.1 7.1 %collective-permute-start.6 = (bf16[16,4096]{1,0:T(8,128)(2,1)S(1)}, bf16[16,4096]{1,0:T(8,128)(2,1)S(1)}, u32[]{:S(2)}, u32[]{:S(2)}) collective-permute-start(bf16[16,4096]{1,0:T(8,128)(2,1)S(1)} %collective-permute-done.5), channel_id=1, source_target_pairs={{0,1},{1,2},{2,3},{3,4},{4,5},{5,6},{6,7},{7,8},{8,9},{9,10},{10,1... | collective-permute-start | bytes 393224 | tf_op jit(solution)/shard_map/ppermute | solution.py:21
  58.2 7.1 %collective-permute-start.7 = (bf16[16,4096]{1,0:T(8,128)(2,1)S(1)}, bf16[16,4096]{1,0:T(8,128)(2,1)S(1)}, u32[]{:S(2)}, u32[]{:S(2)}) collective-permute-start(bf16[16,4096]{1,0:T(8,128)(2,1)S(1)} %collective-permute-done.6), channel_id=1, source_target_pairs={{0,1},{1,2},{2,3},{3,4},{4,5},{5,6},{6,7},{7,8},{8,9},{9,10},{10,1... | collective-permute-start | bytes 393224 | tf_op jit(solution)/shard_map/ppermute | solution.py:21
  58.2 57.2 %copy-start.5 = (f32[1,4096]{1,0:T(1,128)S(1)}, f32[1,4096]{1,0:T(1,128)}, u32[]{:S(2)}) copy-start(f32[1,4096]{1,0:T(1,128)} %param.13) | copy-start | bytes 49156
  65.2 7.1 %collective-permute-start.8 = (bf16[16,4096]{1,0:T(8,128)(2,1)S(1)}, bf16[16,4096]{1,0:T(8,128)(2,1)S(1)}, u32[]{:S(2)}, u32[]{:S(2)}) collective-permute-start(bf16[16,4096]{1,0:T(8,128)(2,1)S(1)} %collective-permute-done.7), channel_id=1, source_target_pairs={{0,1},{1,2},{2,3},{3,4},{4,5},{5,6},{6,7},{7,8},{8,9},{9,10},{10,1... | collective-permute-start | bytes 393224 | tf_op jit(solution)/shard_map/ppermute | solution.py:21
  72.3 7.1 %collective-permute-start.9 = (bf16[16,4096]{1,0:T(8,128)(2,1)S(1)}, bf16[16,4096]{1,0:T(8,128)(2,1)S(1)}, u32[]{:S(2)}, u32[]{:S(2)}) collective-permute-start(bf16[16,4096]{1,0:T(8,128)(2,1)S(1)} %collective-permute-done.8), channel_id=1, source_target_pairs={{0,1},{1,2},{2,3},{3,4},{4,5},{5,6},{6,7},{7,8},{8,9},{9,10},{10,1... | collective-permute-start | bytes 393224 | tf_op jit(solution)/shard_map/ppermute | solution.py:21
  79.4 7.1 %collective-permute-start.10 = (bf16[16,4096]{1,0:T(8,128)(2,1)S(1)}, bf16[16,4096]{1,0:T(8,128)(2,1)S(1)}, u32[]{:S(2)}, u32[]{:S(2)}) collective-permute-start(bf16[16,4096]{1,0:T(8,128)(2,1)S(1)} %collective-permute-done.9), channel_id=1, source_target_pairs={{0,1},{1,2},{2,3},{3,4},{4,5},{5,6},{6,7},{7,8},{8,9},{9,10},{10,1... | collective-permute-start | bytes 393224 | tf_op jit(solution)/shard_map/ppermute | solution.py:21
  86.5 7.1 %collective-permute-start.11 = (bf16[16,4096]{1,0:T(8,128)(2,1)S(1)}, bf16[16,4096]{1,0:T(8,128)(2,1)S(1)}, u32[]{:S(2)}, u32[]{:S(2)}) collective-permute-start(bf16[16,4096]{1,0:T(8,128)(2,1)S(1)} %collective-permute-done.10), channel_id=1, source_target_pairs={{0,1},{1,2},{2,3},{3,4},{4,5},{5,6},{6,7},{7,8},{8,9},{9,10},{10,1... | collective-permute-start | bytes 393224 | tf_op jit(solution)/shard_map/ppermute | solution.py:21
  93.6 7.1 %collective-permute-start.12 = (bf16[16,4096]{1,0:T(8,128)(2,1)S(1)}, bf16[16,4096]{1,0:T(8,128)(2,1)S(1)}, u32[]{:S(2)}, u32[]{:S(2)}) collective-permute-start(bf16[16,4096]{1,0:T(8,128)(2,1)S(1)} %collective-permute-done.11), channel_id=1, source_target_pairs={{0,1},{1,2},{2,3},{3,4},{4,5},{5,6},{6,7},{7,8},{8,9},{9,10},{10,1... | collective-permute-start | bytes 393224 | tf_op jit(solution)/shard_map/ppermute | solution.py:21
  100.7 7.1 %collective-permute-start.13 = (bf16[16,4096]{1,0:T(8,128)(2,1)S(1)}, bf16[16,4096]{1,0:T(8,128)(2,1)S(1)}, u32[]{:S(2)}, u32[]{:S(2)}) collective-permute-start(bf16[16,4096]{1,0:T(8,128)(2,1)S(1)} %collective-permute-done.12), channel_id=1, source_target_pairs={{0,1},{1,2},{2,3},{3,4},{4,5},{5,6},{6,7},{7,8},{8,9},{9,10},{10,1... | collective-permute-start | bytes 393224 | tf_op jit(solution)/shard_map/ppermute | solution.py:21
  107.8 7.1 %collective-permute-start.14 = (bf16[16,4096]{1,0:T(8,128)(2,1)S(1)}, bf16[16,4096]{1,0:T(8,128)(2,1)S(1)}, u32[]{:S(2)}, u32[]{:S(2)}) collective-permute-start(bf16[16,4096]{1,0:T(8,128)(2,1)S(1)} %collective-permute-done.13), channel_id=1, source_target_pairs={{0,1},{1,2},{2,3},{3,4},{4,5},{5,6},{6,7},{7,8},{8,9},{9,10},{10,1... | collective-permute-start | bytes 393224 | tf_op jit(solution)/shard_map/ppermute | solution.py:21
  161.3 43.7 %copy-start.4 = (s32[128]{0:T(128)S(1)}, s32[128]{0:T(128)}, u32[]{:S(2)}) copy-start(s32[128]{0:T(128)} %param.19) | copy-start | bytes 1540
  161.3 115.8 %reduce-scatter.2.cloned.1.call-start = ((), (), s32[]{:S(2)}) async-start(), calls=%async_computation.4 | async-start | bytes 2228224 | tf_op jit(solution)/shard_map/reduce_scatter | solution.py:98
  215.2 18.1 %all-to-all-start = ((bf16[128,2,2048]{0,2,1:T(8,128)(2,1)}), bf16[128,2,2048]{0,2,1:T(8,128)(2,1)S(1)}, u32[]{:S(2)}, u32[]{:S(2)}) async-start(bf16[128,2,2048]{0,2,1:T(8,128)(2,1)} %bitcast.4), calls=%async_computation | async-start | bytes 2097152 | tf_op jit(solution)/shard_map/all_to_all | solution.py:111
  (1 other events, 0.9 us)
Sparse Core Ops, SparseCore 0:
  9.5 132.1 all-gather.9
  161.4 43.5 all-reduce.1
  215.3 61.7 reduce-scatter.1
